TPU v7x, 256 devices: a whole 4x4x8 slice. The times are simulated.
256 devices in a mesh: seq: 4 (over x), head: 4 (over y), rows: 16 (over z, core).
Axes of the slice: x: 4, y: 4, z: 8, core: 2. Of those that a mesh axis runs over, the one named last changes fastest.
Arguments:
- queries: bfloat16 [8, 4, 5120, 2048], P('seq', None, 'rows', 'head'), may hold values from -6 to 6
- keys: bfloat16 [8, 4, 5120, 2048], P('seq', None, 'rows', 'head'), may hold values from -6 to 6
- values: bfloat16 [8, 4, 5120, 2048], P('seq', None, 'rows', 'head'), may hold values from -6 to 6
- counts: int32 [8], replicated, may hold values from 1 to 4, as said below
- rate: float32 [4], P('head'), may hold values from 0.125 to 1
- w_first: bfloat16 [4, 512, 256], P('head'), may hold values from -0.25 to 0.25
- w_third: bfloat16 [4, 512, 256], P('head'), may hold values from -0.25 to 0.25
- w_second: bfloat16 [4, 256, 512], P('head'), may hold values from -0.375 to 0.375
Outputs:
- mixed: bfloat16 [8, 4, 5120, 2048], P('seq', None, 'rows', 'head')
Inputs may be any that keep to these rules, and one draw needn't show every extreme that they name: `counts`: taken in order, the sequences fall into consecutive runs, as many as there are groups of 2 sequences, each run with exactly 4 blocks in all; some sequence has 4 blocks.
All inputs are finite; a program needn't handle non-finite values.
Results may differ from a plain program's by a relative error of at most 0.02.
Values may be sent and summed in bfloat16 or wider, within the bound.
No kernel may reach another device: no remote copies, remote signals or barrier semaphores. Data moves between devices by JAX's collectives and lax.ppermute only.
A program may use at most 64 MiB of HBM per device.

v0:
```python
import jax
import jax.numpy as jnp
from jax import lax
from jax.sharding import PartitionSpec as P


def normalize_rows(matrix, epsilon):
    matrix = matrix.astype(jnp.float32)
    return matrix * lax.rsqrt(jnp.mean(matrix * matrix, axis=-1, keepdims=True) + epsilon)


def column_norms(weight):
    return jnp.sqrt(jnp.sum(weight * weight, axis=0) + 1e-06)


def rescale(moved, target):
    return moved * (target[None, :] / column_norms(moved)[None, :])


def product(first_op, second_op):
    return jnp.dot(first_op, second_op, preferred_element_type=jnp.float32)


def contract_rows(first_op, second_op):
    return lax.dot_general(
        first_op, second_op, (((0,), (0,)), ((), ())), preferred_element_type=jnp.float32
    )


def against_rows(first_op, second_op):
    return lax.dot_general(
        first_op, second_op, (((1,), (1,)), ((), ())), preferred_element_type=jnp.float32
    )


def partial_sums(current, key_rows, value_rows):
    key_norm = normalize_rows(key_rows, 1e-06).astype(jnp.bfloat16)
    gate_pre = product(key_norm, current[0])
    up_pre = product(key_norm, current[1])
    gate_sig = jax.nn.sigmoid(gate_pre)
    gate_act = gate_pre * gate_sig
    hidden = (gate_act * up_pre).astype(jnp.bfloat16)
    d_hidden = against_rows(value_rows, current[2])
    d_gate = (d_hidden * up_pre * gate_sig * (1.0 + gate_pre * (1.0 - gate_sig))).astype(
        jnp.bfloat16
    )
    d_up = (d_hidden * gate_act).astype(jnp.bfloat16)
    return (
        contract_rows(key_norm, d_gate),
        contract_rows(key_norm, d_up),
        contract_rows(hidden, value_rows),
    )


def answer(current, query_rows):
    query_norm = normalize_rows(query_rows, 1e-06).astype(jnp.bfloat16)
    out_gate = product(query_norm, current[0])
    out_up = product(query_norm, current[1])
    out_hidden = (out_gate * jax.nn.sigmoid(out_gate) * out_up).astype(jnp.bfloat16)
    return normalize_rows(product(out_hidden, current[2]), 1e-05).astype(jnp.bfloat16)


def body(queries, keys, values, counts, rate, w_first, w_third, w_second):
    seq_slots, blocks, block_rows, head_width = queries.shape
    group_index = lax.axis_index("seq")
    row_devices = lax.axis_size("rows")
    step_rate = rate[0] / (block_rows * row_devices)
    initial = (w_first[0], w_third[0], w_second[0])
    full_master = tuple((weight.astype(jnp.float32) for weight in initial))
    full_targets = tuple((column_norms(weight) for weight in full_master))

    def combine(partials):
        return (
            lax.psum(partials[0].astype(jnp.bfloat16), "rows").astype(jnp.float32),
            lax.psum(partials[1].astype(jnp.bfloat16), "rows").astype(jnp.float32),
            lax.psum(partials[2].astype(jnp.bfloat16), "rows").astype(jnp.float32),
        )

    def refresh(master):
        as_bf16 = tuple((weight.astype(jnp.bfloat16) for weight in master))
        return as_bf16

    def advance(state_pair, step_inputs):
        master, current = state_pair
        query_rows, key_rows, value_rows, restart, is_live = step_inputs
        master = tuple(
            (
                jnp.where(restart, fresh_value, kept_value)
                for fresh_value, kept_value in zip(full_master, master)
            )
        )
        current = tuple(
            (
                jnp.where(restart, fresh_value, kept_value)
                for fresh_value, kept_value in zip(initial, current)
            )
        )
        totals = combine(partial_sums(current, key_rows, value_rows))
        moved = tuple(
            (
                rescale(weight + step_rate * grad_total, target)
                for weight, grad_total, target in zip(master, totals, full_targets)
            )
        )
        master = tuple((jnp.where(is_live, new_w, old_w) for new_w, old_w in zip(moved, master)))
        current = refresh(master)
        output = answer(current, query_rows)
        return ((master, current), jnp.where(is_live, output, jnp.zeros_like(output)))

    start_pair = (full_master, initial)
    flat_shape = (seq_slots * blocks, block_rows, head_width)
    block_ids = jnp.arange(blocks, dtype=jnp.int32)
    local_counts = lax.dynamic_slice_in_dim(counts, group_index * seq_slots, seq_slots)
    restart = jnp.tile(block_ids == 0, seq_slots)
    is_live = (block_ids[None, :] < local_counts[:, None]).reshape(-1)
    inputs = (
        queries.reshape(flat_shape),
        keys.reshape(flat_shape),
        values.reshape(flat_shape),
        restart,
        is_live,
    )
    _, outputs = lax.scan(advance, start_pair, inputs)
    return outputs.reshape(queries.shape)


def solution(mesh):
    return jax.shard_map(
        body,
        mesh=mesh,
        in_specs=(
            P("seq", None, "rows", "head"),
            P("seq", None, "rows", "head"),
            P("seq", None, "rows", "head"),
            P(),
            P("head"),
            P("head", None, None),
            P("head", None, None),
            P("head", None, None),
        ),
        out_specs=P("seq", None, "rows", "head"),
        check_vma=False,
    )
```

profile of v0, /device:TPU:5, one launch (start us, length us, event | category | flops | bytes accessed | tf_op | source)
XLA Modules:
  0.0 1177.6 jit_solution(11395213980527724467)
XLA Ops:
  16.9 1153.8 %while.22 = (s32[]{:T(128)}, f32[512,256]{1,0:T(8,128)S(1)}, f32[512,256]{1,0:T(8,128)S(1)}, f32[256,512]{1,0:T(8,128)S(1)}, bf16[512,256]{1,0:T(8,128)(2,1)S(1)...) while((s32[]{:T(128)}, f32[512,256]{1,0:T(8,128)S(1)}, ...), condition=%wide.region_13.14_spmd, body=%wide.region_3.13_spmd.sunk | while | flops 768313280 | bytes 32221672 | solution.py:123
  26.8 2.2 convolution_convert_fusion.6
  32.9 113.1 %all-reduce.5.cloned.1.call-done = (bf16[512,256]{1,0:T(8,128)(2,1)}, bf16[512,256]{1,0:T(8,128)(2,1)}, bf16[256,512]{1,0:T(8,128)(2,1)}) async-done(((bf16[512,256]{1,0:T(8,128)(2,1)}, bf16[512,256]{1,0:T(8,128)(2,1)}, bf16[256,512]{1,0:T(8,128)(2,1)}), (bf16[512,256]{1,0:T(8,128)(2,1)}, bf16[512,256]{1,0:T(8,128)(2,1)}, bf16[256,512]{1,0:T(8,128)(2,1)})) %all-reduce.5.cloned.1.call-update) | async-done | bytes 786448 | tf_op jit(solution)/shard_map/while/body/eval_jaxpr/psum | solution.py:74
  149.8 2.4 fusion.101
  152.2 2.4 fusion.100
  158.3 2.6 multiply_reduce_fusion.12
  160.9 2.6 fusion.104
  173.1 2.2 convolution_convert_fusion.6
  179.2 110.7 %all-reduce.5.cloned.1.call-done = (bf16[512,256]{1,0:T(8,128)(2,1)}, bf16[512,256]{1,0:T(8,128)(2,1)}, bf16[256,512]{1,0:T(8,128)(2,1)}) async-done(((bf16[512,256]{1,0:T(8,128)(2,1)}, bf16[512,256]{1,0:T(8,128)(2,1)}, bf16[256,512]{1,0:T(8,128)(2,1)}), (bf16[512,256]{1,0:T(8,128)(2,1)}, bf16[512,256]{1,0:T(8,128)(2,1)}, bf16[256,512]{1,0:T(8,128)(2,1)})) %all-reduce.5.cloned.1.call-update) | async-done | bytes 786448 | tf_op jit(solution)/shard_map/while/body/eval_jaxpr/psum | solution.py:74
  293.7 2.4 fusion.101
  296.1 2.4 fusion.100
  302.2 2.6 multiply_reduce_fusion.12
  304.8 2.6 fusion.104
  317.0 2.2 convolution_convert_fusion.6
  323.1 110.7 %all-reduce.5.cloned.1.call-done = (bf16[512,256]{1,0:T(8,128)(2,1)}, bf16[512,256]{1,0:T(8,128)(2,1)}, bf16[256,512]{1,0:T(8,128)(2,1)}) async-done(((bf16[512,256]{1,0:T(8,128)(2,1)}, bf16[512,256]{1,0:T(8,128)(2,1)}, bf16[256,512]{1,0:T(8,128)(2,1)}), (bf16[512,256]{1,0:T(8,128)(2,1)}, bf16[512,256]{1,0:T(8,128)(2,1)}, bf16[256,512]{1,0:T(8,128)(2,1)})) %all-reduce.5.cloned.1.call-update) | async-done | bytes 786448 | tf_op jit(solution)/shard_map/while/body/eval_jaxpr/psum | solution.py:74
  437.6 2.4 fusion.101
  440.0 2.4 fusion.100
  446.1 2.6 multiply_reduce_fusion.12
  448.7 2.6 fusion.104
  460.9 2.2 convolution_convert_fusion.6
  467.1 110.7 %all-reduce.5.cloned.1.call-done = (bf16[512,256]{1,0:T(8,128)(2,1)}, bf16[512,256]{1,0:T(8,128)(2,1)}, bf16[256,512]{1,0:T(8,128)(2,1)}) async-done(((bf16[512,256]{1,0:T(8,128)(2,1)}, bf16[512,256]{1,0:T(8,128)(2,1)}, bf16[256,512]{1,0:T(8,128)(2,1)}), (bf16[512,256]{1,0:T(8,128)(2,1)}, bf16[512,256]{1,0:T(8,128)(2,1)}, bf16[256,512]{1,0:T(8,128)(2,1)})) %all-reduce.5.cloned.1.call-update) | async-done | bytes 786448 | tf_op jit(solution)/shard_map/while/body/eval_jaxpr/psum | solution.py:74
  581.5 2.4 fusion.101
  583.9 2.4 fusion.100
  590.0 2.6 multiply_reduce_fusion.12
  592.6 2.6 fusion.104
  604.9 2.2 convolution_convert_fusion.6
  611.1 110.5 %all-reduce.5.cloned.1.call-done = (bf16[512,256]{1,0:T(8,128)(2,1)}, bf16[512,256]{1,0:T(8,128)(2,1)}, bf16[256,512]{1,0:T(8,128)(2,1)}) async-done(((bf16[512,256]{1,0:T(8,128)(2,1)}, bf16[512,256]{1,0:T(8,128)(2,1)}, bf16[256,512]{1,0:T(8,128)(2,1)}), (bf16[512,256]{1,0:T(8,128)(2,1)}, bf16[512,256]{1,0:T(8,128)(2,1)}, bf16[256,512]{1,0:T(8,128)(2,1)})) %all-reduce.5.cloned.1.call-update) | async-done | bytes 786448 | tf_op jit(solution)/shard_map/while/body/eval_jaxpr/psum | solution.py:74
  725.3 2.4 fusion.101
  727.7 2.4 fusion.100
  733.8 2.6 multiply_reduce_fusion.12
  736.4 2.6 fusion.104
  754.8 110.7 %all-reduce.5.cloned.1.call-done = (bf16[512,256]{1,0:T(8,128)(2,1)}, bf16[512,256]{1,0:T(8,128)(2,1)}, bf16[256,512]{1,0:T(8,128)(2,1)}) async-done(((bf16[512,256]{1,0:T(8,128)(2,1)}, bf16[512,256]{1,0:T(8,128)(2,1)}, bf16[256,512]{1,0:T(8,128)(2,1)}), (bf16[512,256]{1,0:T(8,128)(2,1)}, bf16[512,256]{1,0:T(8,128)(2,1)}, bf16[256,512]{1,0:T(8,128)(2,1)})) %all-reduce.5.cloned.1.call-update) | async-done | bytes 786448 | tf_op jit(solution)/shard_map/while/body/eval_jaxpr/psum | solution.py:74
  869.2 2.4 fusion.101
  871.6 2.4 fusion.100
  877.7 2.6 multiply_reduce_fusion.12
  880.3 2.6 fusion.104
  892.6 2.2 convolution_convert_fusion.6
  898.7 110.7 %all-reduce.5.cloned.1.call-done = (bf16[512,256]{1,0:T(8,128)(2,1)}, bf16[512,256]{1,0:T(8,128)(2,1)}, bf16[256,512]{1,0:T(8,128)(2,1)}) async-done(((bf16[512,256]{1,0:T(8,128)(2,1)}, bf16[512,256]{1,0:T(8,128)(2,1)}, bf16[256,512]{1,0:T(8,128)(2,1)}), (bf16[512,256]{1,0:T(8,128)(2,1)}, bf16[512,256]{1,0:T(8,128)(2,1)}, bf16[256,512]{1,0:T(8,128)(2,1)})) %all-reduce.5.cloned.1.call-update) | async-done | bytes 786448 | tf_op jit(solution)/shard_map/while/body/eval_jaxpr/psum | solution.py:74
  1013.1 2.4 fusion.101
  1015.6 2.4 fusion.100
  1021.6 2.6 multiply_reduce_fusion.12
  1024.3 2.6 fusion.104
  1036.5 2.2 convolution_convert_fusion.6
  1042.6 110.7 %all-reduce.5.cloned.1.call-done = (bf16[512,256]{1,0:T(8,128)(2,1)}, bf16[512,256]{1,0:T(8,128)(2,1)}, bf16[256,512]{1,0:T(8,128)(2,1)}) async-done(((bf16[512,256]{1,0:T(8,128)(2,1)}, bf16[512,256]{1,0:T(8,128)(2,1)}, bf16[256,512]{1,0:T(8,128)(2,1)}), (bf16[512,256]{1,0:T(8,128)(2,1)}, bf16[512,256]{1,0:T(8,128)(2,1)}, bf16[256,512]{1,0:T(8,128)(2,1)})) %all-reduce.5.cloned.1.call-update) | async-done | bytes 786448 | tf_op jit(solution)/shard_map/while/body/eval_jaxpr/psum | solution.py:74
  1157.0 2.4 fusion.101
  1159.5 2.4 fusion.100
  1165.5 2.6 multiply_reduce_fusion.12
  1168.2 2.6 fusion.104
  (273 shorter events, 179.6 us)
Async XLA Ops:
  6.5 10.2 copy-start.3
  6.5 10.2 copy-start.4
  17.0 129.1 %all-reduce.5.cloned.1.call-start = ((), (), s32[]{:S(2)}) async-start(), calls=%async_computation | async-start | bytes 1572864 | tf_op jit(solution)/shard_map/while/body/eval_jaxpr/psum | solution.py:74
  17.0 7.9 copy-start.5
  17.0 7.8 copy-start.6
  146.0 3.7 copy-start
  147.8 4.4 copy-start.2
  149.7 4.8 copy-start.1
  163.5 126.5 %all-reduce.5.cloned.1.call-start = ((), (), s32[]{:S(2)}) async-start(), calls=%async_computation | async-start | bytes 1572864 | tf_op jit(solution)/shard_map/while/body/eval_jaxpr/psum | solution.py:74
  163.5 7.8 copy-start.5
  163.5 7.8 copy-start.6
  289.9 3.7 copy-start
  291.7 4.4 copy-start.2
  293.6 4.8 copy-start.1
  307.4 126.5 %all-reduce.5.cloned.1.call-start = ((), (), s32[]{:S(2)}) async-start(), calls=%async_computation | async-start | bytes 1572864 | tf_op jit(solution)/shard_map/while/body/eval_jaxpr/psum | solution.py:74
  307.4 7.8 copy-start.5
  307.4 7.8 copy-start.6
  433.8 3.7 copy-start
  435.6 4.4 copy-start.2
  437.6 4.8 copy-start.1
  451.3 126.5 %all-reduce.5.cloned.1.call-start = ((), (), s32[]{:S(2)}) async-start(), calls=%async_computation | async-start | bytes 1572864 | tf_op jit(solution)/shard_map/while/body/eval_jaxpr/psum | solution.py:74
  451.3 7.8 copy-start.5
  451.3 7.8 copy-start.6
  577.8 3.7 copy-start
  579.5 4.4 copy-start.2
  581.5 4.8 copy-start.1
  595.2 126.3 %all-reduce.5.cloned.1.call-start = ((), (), s32[]{:S(2)}) async-start(), calls=%async_computation | async-start | bytes 1572864 | tf_op jit(solution)/shard_map/while/body/eval_jaxpr/psum | solution.py:74
  595.2 7.8 copy-start.5
  595.2 7.8 copy-start.6
  721.6 3.7 copy-start
  723.3 4.4 copy-start.2
  725.3 4.8 copy-start.1
  739.0 126.5 %all-reduce.5.cloned.1.call-start = ((), (), s32[]{:S(2)}) async-start(), calls=%async_computation | async-start | bytes 1572864 | tf_op jit(solution)/shard_map/while/body/eval_jaxpr/psum | solution.py:74
  739.0 7.8 copy-start.5
  739.0 7.8 copy-start.6
  867.2 4.4 copy-start.2
  869.2 4.8 copy-start.1
  882.9 126.5 %all-reduce.5.cloned.1.call-start = ((), (), s32[]{:S(2)}) async-start(), calls=%async_computation | async-start | bytes 1572864 | tf_op jit(solution)/shard_map/while/body/eval_jaxpr/psum | solution.py:74
  882.9 7.8 copy-start.5
  882.9 7.8 copy-start.6
  1009.4 3.7 copy-start
  1011.2 4.4 copy-start.2
  1013.1 4.8 copy-start.1
  1026.8 126.5 %all-reduce.5.cloned.1.call-start = ((), (), s32[]{:S(2)}) async-start(), calls=%async_computation | async-start | bytes 1572864 | tf_op jit(solution)/shard_map/while/body/eval_jaxpr/psum | solution.py:74
  1026.8 7.8 copy-start.5
  1026.8 7.8 copy-start.6
  1155.1 4.4 copy-start.2
  1157.0 4.8 copy-start.1
  (2 other events, 7.5 us)
Sparse Core Ops, SparseCore 0:
  31.2 114.7 all-reduce.4
  177.6 112.2 all-reduce.4
  321.5 112.2 all-reduce.4
  465.4 112.2 all-reduce.4
  609.4 112.0 all-reduce.4
  753.1 112.2 all-reduce.4
  897.0 112.2 all-reduce.4
  1041.0 112.2 all-reduce.4
where the time goes:
time: 1180 us
  waiting for transfers between devices  888 us (75%)
  matrix products  134 us (11%)
  other arithmetic  125 us (11%)
  local copies, waits for them, and re-layouts  15.6 us (1%)
  between operations  14.2 us (1%)
    psum x8, waiting for transfers between devices, combine(): lax.psum(partials[0].astype(jnp.bfloat16), 'rows').astype(jnp.float32)  888 us
    dot_general x32, matrix products, product(): return jnp.dot(first_op, second_op, preferred_element_type=jnp.float32)  68.3 us
    convert_element_type x24, other arithmetic, refresh(): as_bf16 = tuple((weight.astype(jnp.bfloat16) for weight in master))  51.8 us
    dot_general x24, matrix products, contract_rows(): lax.dot_general(first_op, second_op, (((0,), (0,)), ((), ())), preferred_...  51 us
    reduce_sum x19, other arithmetic, column_norms(): return jnp.sqrt(jnp.sum(weight * weight, axis=0) + 1e-06)  32.7 us
  transfers between devices with their start and end apart: 8, of which 8 were waited for; matrix products, arithmetic and copies ran while one was open for 1% of the time, Pallas kernels for 0%

commit v1 on v0

v1 whole, which is shorter than its diff:
```python
import jax
import jax.numpy as jnp
from jax import lax
from jax.experimental import pallas as pl
from jax.experimental.pallas import tpu as pltpu
from jax.sharding import Mesh, PartitionSpec as P

F32 = jnp.float32
BF16 = jnp.bfloat16
NT = (((1,), (1,)), ((), ()))
NN = (((1,), (0,)), ((), ()))
TN = (((0,), (0,)), ((), ()))


def dot(first_op, second_op, dims):
    return lax.dot_general(first_op, second_op, dims, preferred_element_type=F32)


def normalized(rows, epsilon):
    rows = rows.astype(F32)
    return rows * lax.rsqrt(jnp.mean(rows * rows, axis=-1, keepdims=True) + epsilon)


def weights_of(w_ref, target_ref):
    hidden = w_ref.shape[0] * w_ref.shape[2]
    parts = [w_ref[:, i].reshape(hidden, w_ref.shape[3]) for i in range(3)]
    down = parts[2].astype(F32)
    scale = target_ref[...] / jnp.sqrt(jnp.sum(down * down, axis=0, keepdims=True) + 1e-06)
    return parts[0], parts[1], (down * scale).astype(BF16), scale


def sums_kernel(info, k_ref, v_ref, w_ref, w0_ref, target_ref, own_ref, send_ref, scale_ref, pick_ref):
    restart, core = info[1], info[2]

    @pl.when(restart == 1)
    def _():
        pick_ref[...] = w0_ref[...]

    @pl.when(restart == 0)
    def _():
        pick_ref[...] = w_ref[...]

    gate, up, down, scale = weights_of(pick_ref, target_ref)
    scale_ref[...] = scale
    keys = normalized(k_ref[0], 1e-06).astype(BF16)
    values = v_ref[0]
    gate_pre = dot(keys, gate, NT)
    up_pre = dot(keys, up, NT)
    d_hidden = dot(values, down, NT)
    gate_sig = jax.nn.sigmoid(gate_pre)
    gate_act = gate_pre * gate_sig
    hidden = (gate_act * up_pre).astype(BF16)
    d_gate = (d_hidden * up_pre * gate_sig * (1.0 + gate_pre * (1.0 - gate_sig))).astype(BF16)
    d_up = (d_hidden * gate_act).astype(BF16)
    n, _, rows, width = own_ref.shape
    for i, (left, right) in enumerate(((d_gate, keys), (d_up, keys), (hidden, values))):
        total = dot(left, right, TN).astype(BF16).reshape(n, 2, rows, width)

        @pl.when(core == 0)
        def _():
            own_ref[:, i] = total[:, 0]
            send_ref[:, i] = total[:, 1]

        @pl.when(core == 1)
        def _():
            own_ref[:, i] = total[:, 1]
            send_ref[:, i] = total[:, 0]


def update_kernel(info, step_ref, x_ref, m_ref, m0_ref, scale_ref, goal_ref, w_ref, out_ref):
    keep = info[0] == 0
    total = jnp.sum(x_ref[...].astype(F32), axis=0) * step_ref[0]
    for i in range(3):
        old = jnp.where(keep, m_ref[i], m0_ref[i])
        if i == 2:
            new = old * scale_ref[...] + total[i]
        else:
            moved = old + total[i]
            norm = jnp.sqrt(jnp.sum(moved * moved, axis=1, keepdims=True) + 1e-06)
            new = moved * (goal_ref[i] / norm)
        out_ref[i] = new
        w_ref[i] = new.astype(BF16)


def answer_kernel(info, q_ref, w_ref, target_ref, old_ref, out_ref):
    @pl.when(info[1] == 1)
    def _():
        gate, up, down, _ = weights_of(w_ref, target_ref)
        query = normalized(q_ref[0], 1e-06).astype(BF16)
        out_gate = dot(query, gate, NT)
        out_up = dot(query, up, NT)
        out_hidden = (out_gate * jax.nn.sigmoid(out_gate) * out_up).astype(BF16)
        out_ref[0] = normalized(dot(out_hidden, down, NN), 1e-05).astype(BF16)

    @pl.when(info[1] == 0)
    def _():
        out_ref[0] = jnp.zeros_like(out_ref[0])


def call(kernel, n_scalars, in_specs, out_specs, out_shape, scratch=(), **kw):
    return pl.pallas_call(
        kernel,
        grid_spec=pltpu.PrefetchScalarGridSpec(
            num_scalar_prefetch=n_scalars, grid=(1,), in_specs=in_specs, out_specs=out_specs, scratch_shapes=scratch
        ),
        out_shape=out_shape,
        compiler_params=pltpu.CompilerParams(vmem_limit_bytes=48 << 20),
        **kw,
    )


def whole(shape):
    return pl.BlockSpec(shape, lambda *_: (0,) * len(shape))


def body(queries, keys, values, counts, rate, w_first, w_third, w_second):
    slots, blocks, block_rows, width = queries.shape
    hidden = w_first.shape[2]
    n_z, n_core = lax.axis_size("z"), lax.axis_size("core")
    n_dev = n_z * n_core
    share = hidden // n_dev
    group, core = lax.axis_index("seq"), lax.axis_index("core")
    me = lax.axis_index("z") * n_core + core
    step = (rate / (block_rows * n_dev)).astype(F32)

    flat = (slots * blocks, block_rows, width)
    queries, keys, values = (a.reshape(flat) for a in (queries, keys, values))
    start = jnp.stack([w_first[0].T, w_third[0].T, w_second[0]])
    w0 = start.reshape(3, n_dev, share, width).transpose(1, 0, 2, 3)
    m0 = lax.dynamic_index_in_dim(w0, me, 0, keepdims=False).astype(F32)
    goal = jnp.sqrt(jnp.sum(m0[:2] * m0[:2], axis=2, keepdims=True) + 1e-06)
    second = w_second[0].astype(F32)
    target = jnp.sqrt(jnp.sum(second * second, axis=0, keepdims=True) + 1e-06)

    local = lax.dynamic_slice_in_dim(counts, group * slots, slots)
    first_len, live = local[0], local[0] + local[1]

    def place(t):
        return jnp.where(t < first_len, t, blocks + t - first_len)

    w_shape, m_shape = (n_dev, 3, share, width), (3, share, width)
    half = (n_z, 3, share, width)
    row_block = lambda: pl.BlockSpec((1, block_rows, width), lambda i, info: (info[0], 0, 0))

    def sums(t, w):
        t = jnp.minimum(t, live - 1)
        restart = ((t == 0) | (t == first_len)).astype(jnp.int32)
        info = jnp.stack([place(t), restart, core])
        return call(
            sums_kernel,
            1,
            [row_block(), row_block(), whole(w_shape), whole(w_shape), whole((1, width))],
            [whole(half), whole(half), whole((1, width))],
            [jax.ShapeDtypeStruct(half, BF16), jax.ShapeDtypeStruct(half, BF16), jax.ShapeDtypeStruct((1, width), F32)],
            [pltpu.VMEM(w_shape, BF16)],
        )(info, keys, values, w, w0, target)

    def update(t, x, m, scale):
        restart = ((t == 0) | (t == first_len)).astype(jnp.int32)
        return call(
            update_kernel,
            2,
            [whole(half), whole(m_shape), whole(m_shape), whole((1, width)), whole(goal.shape)],
            [whole(m_shape), whole(m_shape)],
            [jax.ShapeDtypeStruct(m_shape, BF16), jax.ShapeDtypeStruct(m_shape, F32)],
        )(restart[None], step, x, m, m0, scale, goal)

    def answer(t, on, w, out):
        info = jnp.stack([place(t), on.astype(jnp.int32)])
        return call(
            answer_kernel,
            1,
            [row_block(), whole(w_shape), whole((1, width)), pl.BlockSpec(memory_space=pl.ANY)],
            row_block(),
            jax.ShapeDtypeStruct(flat, BF16),
            input_output_aliases={4: 0},
        )(info, queries, w, target, out)

    def advance(t, carry):
        own, send, scale, w, m, out = carry
        got = lax.ppermute(send, "core", [(0, 1), (1, 0)])
        out = answer(jnp.maximum(t - 1, 0), t > 0, w, out)
        pair = (own.astype(F32) + got.astype(F32)).astype(BF16)
        parts = lax.all_to_all(pair, "z", 0, 0, tiled=True)
        chunk, m = update(t, parts, m, scale)
        w = lax.all_gather(chunk, ("z", "core"), axis=0)
        own, send, scale = sums(t + 1, w)
        return own, send, scale, w, m, out

    out = jnp.zeros(flat, BF16)
    own, send, scale = sums(jnp.int32(0), w0)
    carry = lax.fori_loop(0, live, advance, (own, send, scale, w0, m0, out))
    out = answer(live - 1, live > 0, carry[3], carry[5])
    return out.reshape(slots, blocks, block_rows, width)


def solution(mesh):
    seq, head, rows = (mesh.shape[name] for name in ("seq", "head", "rows"))
    split = Mesh(mesh.devices.reshape(seq, head, rows // 2, 2), ("seq", "head", "z", "core"))
    data = P("seq", None, ("z", "core"), "head")
    weight = P("head", None, None)
    return jax.shard_map(
        body,
        mesh=split,
        in_specs=(data, data, data, P(), P("head"), weight, weight, weight),
        out_specs=data,
        check_vma=False,
    )
```

time: 1180 us -> 250 us (0.21)
  waiting for transfers between devices: 888 us -> 49.1 us
  matrix products: 134 us -> 0 us
  other arithmetic: 125 us -> 8.6 us
  blocking collectives: 0 us -> 85.8 us
  Pallas kernels: 0 us -> 44.6 us
  starting transfers between devices: 0.06 us -> 23.4 us
  loops' own time: 0.65 us -> 18.4 us
    psum x8 -> x0, waiting for transfers between devices: 888 us -> none  [combine(): lax.psum(partials[0].astype(jnp.bfloat16), 'rows').astype(jnp.float32)]
    dot_general x64 -> x0, matrix products: 134 us -> none  [the longest x32 68.3 us: product(): return jnp.dot(first_op, second_op, preferred_element_type=jnp.float32)]
    all_gather x0 -> x5, blocking collectives: none -> 85.8 us  [advance(): w = lax.all_gather(chunk, ('z', 'core'), axis=0)]
    reduce_sum x35 -> x2, other arithmetic: 50.7 us -> 0.17 us  [the longest x1 0.09 us: body(): goal = jnp.sqrt(jnp.sum(m0[:2] * m0[:2], axis=2, keepdims=True) + 1e-06)]
    convert_element_type x26 -> x6, other arithmetic: 52.9 us -> 5.28 us  [the longest x5 4.47 us: advance(): pair = (own.astype(F32) + got.astype(F32)).astype(BF16)]
    pallas_call x0 -> x17, Pallas kernels: none -> 44.6 us  [the longest x6 26.4 us: sums(): call(sums_kernel, 1, [row_block(), row_block(), whole(w_shape), whole(w_s...]
    all_to_all x0 -> x5, waiting for transfers between devices: none -> 40.4 us  [advance(): parts = lax.all_to_all(pair, 'z', 0, 0, tiled=True)]
    all_to_all x0 -> x5, starting transfers between devices: none -> 22 us  [advance(): parts = lax.all_to_all(pair, 'z', 0, 0, tiled=True)]
  transfers between devices with their start and end apart: 8 -> 10, of which waited for: 8 -> 10; matrix products, arithmetic and copies ran while one was open for 1% -> 2% of each run, Pallas kernels for 0% -> 5%
where the time goes in v1:
time: 250 us; the launch traced here: 248 us
  blocking collectives  85.8 us (34%)
  waiting for transfers between devices  49.1 us (20%)
  Pallas kernels  44.6 us (18%)
  starting transfers between devices  23.4 us (9%)
  loops' own time  18.4 us (7%)
  local copies, waits for them, and re-layouts  13.3 us (5%)
  other arithmetic  8.6 us (3%)
  between operations  5.03 us (2%)
    all_gather x5, blocking collectives, advance(): w = lax.all_gather(chunk, ('z', 'core'), axis=0)  85.8 us
    all_to_all x5, waiting for transfers between devices, advance(): parts = lax.all_to_all(pair, 'z', 0, 0, tiled=True)  40.4 us
    pallas_call x6, Pallas kernels, sums(): call(sums_kernel, 1, [row_block(), row_block(), whole(w_shape), whole(w_s...  26.4 us
    all_to_all x5, starting transfers between devices, advance(): parts = lax.all_to_all(pair, 'z', 0, 0, tiled=True)  22 us
    another operation x1, loops' own time, body(): carry = lax.fori_loop(0, live, advance, (own, send, scale, w0, m0, out))  18.4 us
    pallas_call x6, Pallas kernels, answer(): call(answer_kernel, 1, [row_block(), whole(w_shape), whole((1, width)), p...  13.8 us
    ppermute x5, waiting for transfers between devices, advance(): got = lax.ppermute(send, 'core', [(0, 1), (1, 0)])  8.69 us
  transfers between devices with their start and end apart: 10, of which 10 were waited for; matrix products, arithmetic and copies ran while one was open for 2% of the time, Pallas kernels for 5%

profile of v1, /device:TPU:5, one launch (start us, length us, event | category | flops | bytes accessed | tf_op | source)
XLA Modules:
  0.0 248.2 jit_solution(16318224641584325005)
XLA Ops:
  4.6 1.1 copy.14
  5.7 1.1 copy.15
  6.8 2.2 pad_maximum_fusion
  9.1 4.5 %shard_map.82 = (bf16[8,3,16,512]{3,2,1,0:T(8,128)(2,1)S(1)}, bf16[8,3,16,512]{3,2,1,0:T(8,128)(2,1)}, f32[1,512]{1,0:T(1,128)S(1)}) custom-call(s32[3]{0:T(128)S(1)} %pad_add_fusion.3.info, bf16[8,320,512]{2,1,0:T(8,128)(2,1)S(1)} %bitcast.51, bf16[8,320,512]{2,1,0:T(8,128)(2,1)} %bitcast.52, bf16[16,3,16,512]{3,2,1,0:T(8,128)(2,1)} %get-tuple-element.514.w_ref.w0_ref, ...), custom_call_target="tpu_custom_call" | custom-call | tf_op jit(solution)/shard_map/pallas_call | solution.py:149
  15.9 2.1 copy.22
  18.9 224.1 %while.23 = (s32[]{:T(128)}, bf16[8,3,16,512]{3,2,1,0:T(8,128)(2,1)S(1)}, bf16[8,3,16,512]{3,2,1,0:T(8,128)(2,1)}, f32[1,512]{1,0:T(1,128)S(1)}, bf16[16,3,16,51...) while((s32[]{:T(128)}, ...), condition=%wide.region_3.4_spmd, body=%wide.region_2.3_spmd.sunk | while | flops 786463 | bytes 8503871 | solution.py:192
  19.7 1.6 collective-permute-done
  21.2 0.9 add_convert_fusion.2
  22.1 8.2 %all-to-all-start = ((bf16[8,3,16,512]{3,2,1,0:T(8,128)(2,1)}), bf16[8,3,16,512]{3,2,1,0:T(8,128)(2,1)S(1)}, u32[]{:S(2)}, u32[]{:S(2)}) async-start(bf16[8,3,16,512]{3,2,1,0:T(8,128)(2,1)} %add_convert_fusion.2), calls=%async_computation | async-start | bytes 786432 | tf_op jit(solution)/shard_map/while/body/all_to_all | solution.py:184
  33.9 0.9 copy.42.m_ref
  34.9 1.8 body.17
  36.8 8.7 %all-to-all-done.x_ref = bf16[8,3,16,512]{3,2,1,0:T(8,128)(2,1)S(1)} async-done(((bf16[8,3,16,512]{3,2,1,0:T(8,128)(2,1)}), bf16[8,3,16,512]{3,2,1,0:T(8,128)(2,1)S(1)}, u32[]{:S(2)}, u32[]{:S(2)}) %all-to-all-start) | async-done | bytes 393248 | tf_op jit(solution)/shard_map/while/body/all_to_all | solution.py:184
  46.3 17.2 %all-gather.2 = bf16[48,16,512]{2,1,0:T(8,128)(2,1)S(1)} all-gather(bf16[3,16,512]{2,1,0:T(8,128)(2,1)S(1)} %get-tuple-element.493), channel_id=2, replica_groups=mesh['seq'=4,'head'=4,'z'=8,'core'=2] {'z','core'}, dimensions={0}, use_global_device_ids=true | all-gather | bytes 835584 | tf_op jit(solution)/shard_map/while/body/all_gather | solution.py:186
  63.5 4.4 %body.16 = (bf16[8,3,16,512]{3,2,1,0:T(8,128)(2,1)S(1)}, bf16[8,3,16,512]{3,2,1,0:T(8,128)(2,1)}, f32[1,512]{1,0:T(1,128)S(1)}) custom-call(s32[3]{0:T(128)S(1)} %pad_add_fusion.6.info, bf16[8,320,512]{2,1,0:T(8,128)(2,1)} %get-tuple-element.558.k_ref, bf16[8,320,512]{2,1,0:T(8,128)(2,1)} %get-tuple-element.559.v_ref, bf16[16,3,16,512]{3,2,1,0:T(8,128)(2,1)S(1)} %bitcast.48, ...), custom_call_target="tpu_custom_call" | custom-call | tf_op jit(solution)/shard_map/while/body/pallas_call | solution.py:149
  68.0 1.8 collective-permute-done
  69.8 0.9 add_convert_fusion.2
  70.7 3.5 %all-to-all-start = ((bf16[8,3,16,512]{3,2,1,0:T(8,128)(2,1)}), bf16[8,3,16,512]{3,2,1,0:T(8,128)(2,1)S(1)}, u32[]{:S(2)}, u32[]{:S(2)}) async-start(bf16[8,3,16,512]{3,2,1,0:T(8,128)(2,1)} %add_convert_fusion.2), calls=%async_computation | async-start | bytes 786432 | tf_op jit(solution)/shard_map/while/body/all_to_all | solution.py:184
  77.8 0.9 copy.42.m_ref
  78.8 2.4 body.17
  81.3 7.9 %all-to-all-done.x_ref = bf16[8,3,16,512]{3,2,1,0:T(8,128)(2,1)S(1)} async-done(((bf16[8,3,16,512]{3,2,1,0:T(8,128)(2,1)}), bf16[8,3,16,512]{3,2,1,0:T(8,128)(2,1)S(1)}, u32[]{:S(2)}, u32[]{:S(2)}) %all-to-all-start) | async-done | bytes 393248 | tf_op jit(solution)/shard_map/while/body/all_to_all | solution.py:184
  90.1 17.2 %all-gather.2 = bf16[48,16,512]{2,1,0:T(8,128)(2,1)S(1)} all-gather(bf16[3,16,512]{2,1,0:T(8,128)(2,1)S(1)} %get-tuple-element.493), channel_id=2, replica_groups=mesh['seq'=4,'head'=4,'z'=8,'core'=2] {'z','core'}, dimensions={0}, use_global_device_ids=true | all-gather | bytes 835584 | tf_op jit(solution)/shard_map/while/body/all_gather | solution.py:186
  107.3 4.4 %body.16 = (bf16[8,3,16,512]{3,2,1,0:T(8,128)(2,1)S(1)}, bf16[8,3,16,512]{3,2,1,0:T(8,128)(2,1)}, f32[1,512]{1,0:T(1,128)S(1)}) custom-call(s32[3]{0:T(128)S(1)} %pad_add_fusion.6.info, bf16[8,320,512]{2,1,0:T(8,128)(2,1)} %get-tuple-element.558.k_ref, bf16[8,320,512]{2,1,0:T(8,128)(2,1)} %get-tuple-element.559.v_ref, bf16[16,3,16,512]{3,2,1,0:T(8,128)(2,1)S(1)} %bitcast.48, ...), custom_call_target="tpu_custom_call" | custom-call | tf_op jit(solution)/shard_map/while/body/pallas_call | solution.py:149
  111.8 1.8 collective-permute-done
  113.6 0.9 add_convert_fusion.2
  114.5 3.5 %all-to-all-start = ((bf16[8,3,16,512]{3,2,1,0:T(8,128)(2,1)}), bf16[8,3,16,512]{3,2,1,0:T(8,128)(2,1)S(1)}, u32[]{:S(2)}, u32[]{:S(2)}) async-start(bf16[8,3,16,512]{3,2,1,0:T(8,128)(2,1)} %add_convert_fusion.2), calls=%async_computation | async-start | bytes 786432 | tf_op jit(solution)/shard_map/while/body/all_to_all | solution.py:184
  121.6 0.9 copy.42.m_ref
  122.6 2.4 body.17
  125.0 7.9 %all-to-all-done.x_ref = bf16[8,3,16,512]{3,2,1,0:T(8,128)(2,1)S(1)} async-done(((bf16[8,3,16,512]{3,2,1,0:T(8,128)(2,1)}), bf16[8,3,16,512]{3,2,1,0:T(8,128)(2,1)S(1)}, u32[]{:S(2)}, u32[]{:S(2)}) %all-to-all-start) | async-done | bytes 393248 | tf_op jit(solution)/shard_map/while/body/all_to_all | solution.py:184
  133.9 17.2 %all-gather.2 = bf16[48,16,512]{2,1,0:T(8,128)(2,1)S(1)} all-gather(bf16[3,16,512]{2,1,0:T(8,128)(2,1)S(1)} %get-tuple-element.493), channel_id=2, replica_groups=mesh['seq'=4,'head'=4,'z'=8,'core'=2] {'z','core'}, dimensions={0}, use_global_device_ids=true | all-gather | bytes 835584 | tf_op jit(solution)/shard_map/while/body/all_gather | solution.py:186
  151.0 4.4 %body.16 = (bf16[8,3,16,512]{3,2,1,0:T(8,128)(2,1)S(1)}, bf16[8,3,16,512]{3,2,1,0:T(8,128)(2,1)}, f32[1,512]{1,0:T(1,128)S(1)}) custom-call(s32[3]{0:T(128)S(1)} %pad_add_fusion.6.info, bf16[8,320,512]{2,1,0:T(8,128)(2,1)} %get-tuple-element.558.k_ref, bf16[8,320,512]{2,1,0:T(8,128)(2,1)} %get-tuple-element.559.v_ref, bf16[16,3,16,512]{3,2,1,0:T(8,128)(2,1)S(1)} %bitcast.48, ...), custom_call_target="tpu_custom_call" | custom-call | tf_op jit(solution)/shard_map/while/body/pallas_call | solution.py:149
  155.6 1.8 collective-permute-done
  157.3 0.9 add_convert_fusion.2
  158.2 3.5 %all-to-all-start = ((bf16[8,3,16,512]{3,2,1,0:T(8,128)(2,1)}), bf16[8,3,16,512]{3,2,1,0:T(8,128)(2,1)S(1)}, u32[]{:S(2)}, u32[]{:S(2)}) async-start(bf16[8,3,16,512]{3,2,1,0:T(8,128)(2,1)} %add_convert_fusion.2), calls=%async_computation | async-start | bytes 786432 | tf_op jit(solution)/shard_map/while/body/all_to_all | solution.py:184
  165.4 0.9 copy.42.m_ref
  166.3 2.4 body.17
  168.8 7.9 %all-to-all-done.x_ref = bf16[8,3,16,512]{3,2,1,0:T(8,128)(2,1)S(1)} async-done(((bf16[8,3,16,512]{3,2,1,0:T(8,128)(2,1)}), bf16[8,3,16,512]{3,2,1,0:T(8,128)(2,1)S(1)}, u32[]{:S(2)}, u32[]{:S(2)}) %all-to-all-start) | async-done | bytes 393248 | tf_op jit(solution)/shard_map/while/body/all_to_all | solution.py:184
  177.6 17.2 %all-gather.2 = bf16[48,16,512]{2,1,0:T(8,128)(2,1)S(1)} all-gather(bf16[3,16,512]{2,1,0:T(8,128)(2,1)S(1)} %get-tuple-element.493), channel_id=2, replica_groups=mesh['seq'=4,'head'=4,'z'=8,'core'=2] {'z','core'}, dimensions={0}, use_global_device_ids=true | all-gather | bytes 835584 | tf_op jit(solution)/shard_map/while/body/all_gather | solution.py:186
  194.8 4.4 %body.16 = (bf16[8,3,16,512]{3,2,1,0:T(8,128)(2,1)S(1)}, bf16[8,3,16,512]{3,2,1,0:T(8,128)(2,1)}, f32[1,512]{1,0:T(1,128)S(1)}) custom-call(s32[3]{0:T(128)S(1)} %pad_add_fusion.6.info, bf16[8,320,512]{2,1,0:T(8,128)(2,1)} %get-tuple-element.558.k_ref, bf16[8,320,512]{2,1,0:T(8,128)(2,1)} %get-tuple-element.559.v_ref, bf16[16,3,16,512]{3,2,1,0:T(8,128)(2,1)S(1)} %bitcast.48, ...), custom_call_target="tpu_custom_call" | custom-call | tf_op jit(solution)/shard_map/while/body/pallas_call | solution.py:149
  199.3 1.8 collective-permute-done
  201.1 0.9 add_convert_fusion.2
  202.0 3.5 %all-to-all-start = ((bf16[8,3,16,512]{3,2,1,0:T(8,128)(2,1)}), bf16[8,3,16,512]{3,2,1,0:T(8,128)(2,1)S(1)}, u32[]{:S(2)}, u32[]{:S(2)}) async-start(bf16[8,3,16,512]{3,2,1,0:T(8,128)(2,1)} %add_convert_fusion.2), calls=%async_computation | async-start | bytes 786432 | tf_op jit(solution)/shard_map/while/body/all_to_all | solution.py:184
  209.1 0.9 copy.42.m_ref
  210.1 2.4 body.17
  212.6 7.9 %all-to-all-done.x_ref = bf16[8,3,16,512]{3,2,1,0:T(8,128)(2,1)S(1)} async-done(((bf16[8,3,16,512]{3,2,1,0:T(8,128)(2,1)}), bf16[8,3,16,512]{3,2,1,0:T(8,128)(2,1)S(1)}, u32[]{:S(2)}, u32[]{:S(2)}) %all-to-all-start) | async-done | bytes 393248 | tf_op jit(solution)/shard_map/while/body/all_to_all | solution.py:184
  221.4 17.2 %all-gather.2 = bf16[48,16,512]{2,1,0:T(8,128)(2,1)S(1)} all-gather(bf16[3,16,512]{2,1,0:T(8,128)(2,1)S(1)} %get-tuple-element.493), channel_id=2, replica_groups=mesh['seq'=4,'head'=4,'z'=8,'core'=2] {'z','core'}, dimensions={0}, use_global_device_ids=true | all-gather | bytes 835584 | tf_op jit(solution)/shard_map/while/body/all_gather | solution.py:186
  238.6 4.4 %body.16 = (bf16[8,3,16,512]{3,2,1,0:T(8,128)(2,1)S(1)}, bf16[8,3,16,512]{3,2,1,0:T(8,128)(2,1)}, f32[1,512]{1,0:T(1,128)S(1)}) custom-call(s32[3]{0:T(128)S(1)} %pad_add_fusion.6.info, bf16[8,320,512]{2,1,0:T(8,128)(2,1)} %get-tuple-element.558.k_ref, bf16[8,320,512]{2,1,0:T(8,128)(2,1)} %get-tuple-element.559.v_ref, bf16[16,3,16,512]{3,2,1,0:T(8,128)(2,1)S(1)} %bitcast.48, ...), custom_call_target="tpu_custom_call" | custom-call | tf_op jit(solution)/shard_map/while/body/pallas_call | solution.py:149
  244.3 2.4 shard_map.83
  246.7 1.5 copy-done
  (59 shorter events, 10.8 us)
Async XLA Ops:
  0.0 9.0 %copy-start.5 = (bf16[1,256,512]{2,1,0:T(8,128)(2,1)S(1)}, bf16[1,256,512]{2,1,0:T(8,128)(2,1)}, u32[]{:S(2)}) copy-start(bf16[1,256,512]{2,1,0:T(8,128)(2,1)} %param.17) | copy-start | bytes 786436
  0.0 9.1 %copy-start.2 = (bf16[2,4,320,512]{3,2,1,0:T(8,128)(2,1)S(1)}, bf16[2,4,320,512]{3,2,1,0:T(8,128)(2,1)}, u32[]{:S(2)}) copy-start(bf16[2,4,320,512]{3,2,1,0:T(8,128)(2,1)} %param.11) | copy-start | bytes 7864324
  14.4 0.7 copy-start.3
  18.9 2.3 collective-permute-start
  22.1 23.3 %all-to-all-start = ((bf16[8,3,16,512]{3,2,1,0:T(8,128)(2,1)}), bf16[8,3,16,512]{3,2,1,0:T(8,128)(2,1)S(1)}, u32[]{:S(2)}, u32[]{:S(2)}) async-start(bf16[8,3,16,512]{3,2,1,0:T(8,128)(2,1)} %add_convert_fusion.2), calls=%async_computation | async-start | bytes 786432 | tf_op jit(solution)/shard_map/while/body/all_to_all | solution.py:184
  34.9 10.5 %copy-start.4 = (f32[3,16,512]{2,1,0:T(8,128)S(1)}, f32[3,16,512]{2,1,0:T(8,128)}, u32[]{:S(2)}) copy-start(f32[3,16,512]{2,1,0:T(8,128)} %get-tuple-element.556.m0_ref) | copy-start | bytes 294916 | tf_op jit(solution)/shard_map/while
  63.5 4.4 %copy-start.1 = (bf16[48,16,512]{2,1,0:T(8,128)(2,1)}, bf16[48,16,512]{2,1,0:T(8,128)(2,1)S(1)}, u32[]{:S(2)}) copy-start(bf16[48,16,512]{2,1,0:T(8,128)(2,1)S(1)} %all-gather.2) | copy-start | bytes 2359300 | tf_op jit(solution)/shard_map/while
  67.9 1.9 collective-permute-start
  70.7 18.5 %all-to-all-start = ((bf16[8,3,16,512]{3,2,1,0:T(8,128)(2,1)}), bf16[8,3,16,512]{3,2,1,0:T(8,128)(2,1)S(1)}, u32[]{:S(2)}, u32[]{:S(2)}) async-start(bf16[8,3,16,512]{3,2,1,0:T(8,128)(2,1)} %add_convert_fusion.2), calls=%async_computation | async-start | bytes 786432 | tf_op jit(solution)/shard_map/while/body/all_to_all | solution.py:184
  78.8 10.4 %copy-start.4 = (f32[3,16,512]{2,1,0:T(8,128)S(1)}, f32[3,16,512]{2,1,0:T(8,128)}, u32[]{:S(2)}) copy-start(f32[3,16,512]{2,1,0:T(8,128)} %get-tuple-element.556.m0_ref) | copy-start | bytes 294916 | tf_op jit(solution)/shard_map/while
  107.2 4.4 %copy-start.1 = (bf16[48,16,512]{2,1,0:T(8,128)(2,1)}, bf16[48,16,512]{2,1,0:T(8,128)(2,1)S(1)}, u32[]{:S(2)}) copy-start(bf16[48,16,512]{2,1,0:T(8,128)(2,1)S(1)} %all-gather.2) | copy-start | bytes 2359300 | tf_op jit(solution)/shard_map/while
  111.6 1.9 collective-permute-start
  114.5 18.5 %all-to-all-start = ((bf16[8,3,16,512]{3,2,1,0:T(8,128)(2,1)}), bf16[8,3,16,512]{3,2,1,0:T(8,128)(2,1)S(1)}, u32[]{:S(2)}, u32[]{:S(2)}) async-start(bf16[8,3,16,512]{3,2,1,0:T(8,128)(2,1)} %add_convert_fusion.2), calls=%async_computation | async-start | bytes 786432 | tf_op jit(solution)/shard_map/while/body/all_to_all | solution.py:184
  122.5 10.4 %copy-start.4 = (f32[3,16,512]{2,1,0:T(8,128)S(1)}, f32[3,16,512]{2,1,0:T(8,128)}, u32[]{:S(2)}) copy-start(f32[3,16,512]{2,1,0:T(8,128)} %get-tuple-element.556.m0_ref) | copy-start | bytes 294916 | tf_op jit(solution)/shard_map/while
  151.0 4.4 %copy-start.1 = (bf16[48,16,512]{2,1,0:T(8,128)(2,1)}, bf16[48,16,512]{2,1,0:T(8,128)(2,1)S(1)}, u32[]{:S(2)}) copy-start(bf16[48,16,512]{2,1,0:T(8,128)(2,1)S(1)} %all-gather.2) | copy-start | bytes 2359300 | tf_op jit(solution)/shard_map/while
  155.4 1.9 collective-permute-start
  158.2 18.5 %all-to-all-start = ((bf16[8,3,16,512]{3,2,1,0:T(8,128)(2,1)}), bf16[8,3,16,512]{3,2,1,0:T(8,128)(2,1)S(1)}, u32[]{:S(2)}, u32[]{:S(2)}) async-start(bf16[8,3,16,512]{3,2,1,0:T(8,128)(2,1)} %add_convert_fusion.2), calls=%async_computation | async-start | bytes 786432 | tf_op jit(solution)/shard_map/while/body/all_to_all | solution.py:184
  166.3 10.4 %copy-start.4 = (f32[3,16,512]{2,1,0:T(8,128)S(1)}, f32[3,16,512]{2,1,0:T(8,128)}, u32[]{:S(2)}) copy-start(f32[3,16,512]{2,1,0:T(8,128)} %get-tuple-element.556.m0_ref) | copy-start | bytes 294916 | tf_op jit(solution)/shard_map/while
  194.8 4.4 %copy-start.1 = (bf16[48,16,512]{2,1,0:T(8,128)(2,1)}, bf16[48,16,512]{2,1,0:T(8,128)(2,1)S(1)}, u32[]{:S(2)}) copy-start(bf16[48,16,512]{2,1,0:T(8,128)(2,1)S(1)} %all-gather.2) | copy-start | bytes 2359300 | tf_op jit(solution)/shard_map/while
  199.2 1.9 collective-permute-start
  202.0 18.5 %all-to-all-start = ((bf16[8,3,16,512]{3,2,1,0:T(8,128)(2,1)}), bf16[8,3,16,512]{3,2,1,0:T(8,128)(2,1)S(1)}, u32[]{:S(2)}, u32[]{:S(2)}) async-start(bf16[8,3,16,512]{3,2,1,0:T(8,128)(2,1)} %add_convert_fusion.2), calls=%async_computation | async-start | bytes 786432 | tf_op jit(solution)/shard_map/while/body/all_to_all | solution.py:184
  210.1 10.4 %copy-start.4 = (f32[3,16,512]{2,1,0:T(8,128)S(1)}, f32[3,16,512]{2,1,0:T(8,128)}, u32[]{:S(2)}) copy-start(f32[3,16,512]{2,1,0:T(8,128)} %get-tuple-element.556.m0_ref) | copy-start | bytes 294916 | tf_op jit(solution)/shard_map/while
  238.6 4.4 %copy-start.1 = (bf16[48,16,512]{2,1,0:T(8,128)(2,1)}, bf16[48,16,512]{2,1,0:T(8,128)(2,1)S(1)}, u32[]{:S(2)}) copy-start(bf16[48,16,512]{2,1,0:T(8,128)(2,1)S(1)} %all-gather.2) | copy-start | bytes 2359300 | tf_op jit(solution)/shard_map/while
  246.7 1.5 copy-start

commit v2 on v1

v2 whole, which is shorter than its diff:
```python
import functools

import jax
import jax.numpy as jnp
from jax import lax
from jax.experimental import pallas as pl
from jax.experimental.pallas import tpu as pltpu
from jax.sharding import Mesh, PartitionSpec as P


F32 = jnp.float32
BF16 = jnp.bfloat16
NT = (((1,), (1,)), ((), ()))
NN = (((1,), (0,)), ((), ()))
TN = (((0,), (0,)), ((), ()))


def dot(first_op, second_op, dims):
    return lax.dot_general(first_op, second_op, dims, preferred_element_type=F32)


def normalized(rows, epsilon):
    rows = rows.astype(F32)
    return rows * lax.rsqrt(jnp.mean(rows * rows, axis=-1, keepdims=True) + epsilon)


def weights_of(w_ref, target_ref):
    parts = [w_ref[:, i].reshape(-1, w_ref.shape[3]) for i in range(3)]
    down = parts[2].astype(F32)
    scale = target_ref[...] / jnp.sqrt(jnp.sum(down * down, axis=0, keepdims=True) + 1e-06)
    return parts[0], parts[1], (down * scale).astype(BF16), scale


def init_kernel(counts, gate_ref, up_ref, down_ref, w_ref, chunk_ref, m_ref, goal_ref, target_ref, meta_ref, *, blocks, slots):
    core = lax.axis_index("core")
    me = lax.axis_index("z") * lax.axis_size("core") + core
    first = lax.axis_index("seq") * slots
    n_first, n_second = counts[first], counts[first + 1]
    second_longer = n_second > n_first
    meta_ref[0] = jnp.where(second_longer, blocks, 0)
    meta_ref[1] = jnp.maximum(n_first, n_second)
    meta_ref[2] = jnp.where(second_longer, 0, blocks)
    meta_ref[3] = jnp.minimum(n_first, n_second)
    meta_ref[4] = core
    n_dev, _, share, width = w_ref.shape
    down = down_ref[0]
    for i, part in enumerate((gate_ref[0].astype(F32).T.astype(BF16), up_ref[0].astype(F32).T.astype(BF16), down)):
        w_ref[:, i] = part.reshape(n_dev, share, width)
    down = down.astype(F32)
    target_ref[...] = jnp.sqrt(jnp.sum(down * down, axis=0, keepdims=True) + 1e-06)
    mine = w_ref[me]
    chunk_ref[...] = mine
    mine = mine.astype(F32)
    m_ref[...] = mine
    for i in range(2):
        goal_ref[i] = jnp.sqrt(jnp.sum(mine[i] * mine[i], axis=1, keepdims=True) + 1e-06)


def sums_kernel(t, meta, k_ref, v_ref, w_ref, target_ref, keep_ref, send_ref, scale_ref):
    core = meta[4]
    gate, up, down, scale = weights_of(w_ref, target_ref)
    scale_ref[...] = scale
    keys = normalized(k_ref[0], 1e-06).astype(BF16)
    values = v_ref[0]
    gate_pre = dot(keys, gate, NT)
    up_pre = dot(keys, up, NT)
    d_hidden = dot(values, down, NT)
    gate_sig = jax.nn.sigmoid(gate_pre)
    gate_act = gate_pre * gate_sig
    hidden = (gate_act * up_pre).astype(BF16)
    d_gate = (d_hidden * up_pre * gate_sig * (1.0 + gate_pre * (1.0 - gate_sig))).astype(BF16)
    d_up = (d_hidden * gate_act).astype(BF16)
    n, _, rows, width = keep_ref.shape
    for i, (left, right) in enumerate(((d_gate, keys), (d_up, keys), (hidden, values))):
        total = dot(left, right, TN).astype(BF16).reshape(n, 2, rows, width)

        @pl.when(core == 0)
        def _():
            keep_ref[:, i] = total[:, 0]
            send_ref[:, i] = total[:, 1]

        @pl.when(core == 1)
        def _():
            keep_ref[:, i] = total[:, 1]
            send_ref[:, i] = total[:, 0]


def update_kernel(step_ref, x_ref, m_ref, scale_ref, goal_ref, w_ref, out_ref):
    total = jnp.sum(x_ref[...].astype(F32), axis=0) * step_ref[0]
    for i in range(3):
        if i == 2:
            new = m_ref[i] * scale_ref[...] + total[i]
        else:
            moved = m_ref[i] + total[i]
            norm = jnp.sqrt(jnp.sum(moved * moved, axis=1, keepdims=True) + 1e-06)
            new = moved * (goal_ref[i] / norm)
        out_ref[i] = new
        w_ref[i] = new.astype(BF16)


def answer_kernel(t, meta, q_ref, w_ref, target_ref, old_ref, out_ref, *, chain, shift):
    at = t[0] - shift
    live = (at >= 0) & (at < meta[2 * chain + 1])

    @pl.when(live)
    def _():
        gate, up, down, _ = weights_of(w_ref, target_ref)
        query = normalized(q_ref[0], 1e-06).astype(BF16)
        out_gate = dot(query, gate, NT)
        out_up = dot(query, up, NT)
        out_hidden = (out_gate * jax.nn.sigmoid(out_gate) * out_up).astype(BF16)
        out_ref[0] = normalized(dot(out_hidden, down, NN), 1e-05).astype(BF16)

    @pl.when(jnp.logical_not(live))
    def _():
        out_ref[0] = jnp.zeros_like(out_ref[0])


def call(kernel, n_scalars, in_specs, out_specs, out_shape, cost=None, **kw):
    return pl.pallas_call(
        kernel,
        grid_spec=pltpu.PrefetchScalarGridSpec(
            num_scalar_prefetch=n_scalars, grid=(1,), in_specs=in_specs, out_specs=out_specs
        ),
        out_shape=out_shape,
        compiler_params=pltpu.CompilerParams(vmem_limit_bytes=40 << 20),
        cost_estimate=cost,
        **kw,
    )


def whole(shape):
    return pl.BlockSpec(shape, lambda *_: (0,) * len(shape))


def body(queries, keys, values, counts, rate, w_first, w_third, w_second):
    slots, blocks, block_rows, width = queries.shape
    hidden = w_first.shape[2]
    n_z, n_core = lax.axis_size("z"), lax.axis_size("core")
    n_dev = n_z * n_core
    share = hidden // n_dev
    step = (rate / (block_rows * n_dev)).astype(F32)
    flat = (slots * blocks, block_rows, width)
    queries, keys, values = (a.reshape(flat) for a in (queries, keys, values))
    w_shape, half, m_shape = (n_dev, 3, share, width), (n_z, 3, share, width), (3, share, width)
    goal_shape, line = (2, share, 1), (1, width)
    shape = jax.ShapeDtypeStruct
    heavy = pl.CostEstimate(flops=2 * 3 * 2 * block_rows * width * hidden, transcendentals=0, bytes_accessed=6 << 20)

    w_init, chunk, m_init, goal, target, meta = call(
        functools.partial(init_kernel, blocks=blocks, slots=slots),
        1,
        [whole((1, width, hidden)), whole((1, width, hidden)), whole((1, hidden, width))],
        [whole(w_shape), whole(m_shape), whole(m_shape), whole(goal_shape), whole(line), pl.BlockSpec(memory_space=pltpu.SMEM)],
        [shape(w_shape, BF16), shape(m_shape, BF16), shape(m_shape, F32), shape(goal_shape, F32), shape(line, F32), shape((8,), jnp.int32)],
    )(counts, w_first, w_third, w_second)
    longest, shortest = meta[1], meta[3]

    def row_block(chain, shift):
        index = lambda i, t, meta: (meta[2 * chain] + jnp.clip(t[0] - shift, 0, blocks - 1), 0, 0)
        return pl.BlockSpec((1, block_rows, width), index)

    def sums(chain, t, shift, w):
        keep, send, scale = call(
            sums_kernel,
            2,
            [row_block(chain, shift), row_block(chain, shift), whole(w_shape), whole(line)],
            [whole(half), whole(half), whole(line)],
            [shape(half, BF16), shape(half, BF16), shape(line, F32)],
            heavy,
        )(t, meta, keys, values, w, target)
        got = lax.ppermute(send, "core", [(0, 1), (1, 0)])
        return (keep.astype(F32) + got.astype(F32)).astype(BF16), scale

    def reduce(pair):
        return lax.all_to_all(pair, "z", 0, 0, tiled=True)

    def update(x, m, scale):
        return call(
            update_kernel,
            1,
            [whole(half), whole(m_shape), whole(line), whole(goal_shape)],
            [whole(m_shape), whole(m_shape)],
            [shape(m_shape, BF16), shape(m_shape, F32)],
        )(step, x, m, scale, goal)

    def gather(chunk):
        return lax.all_gather(chunk, ("z", "core"), axis=0)

    def answer(chain, t, shift, w, out):
        return call(
            functools.partial(answer_kernel, chain=chain, shift=shift),
            2,
            [row_block(chain, shift), whole(w_shape), whole(line), pl.BlockSpec(memory_space=pl.ANY)],
            row_block(chain, shift),
            shape(flat, BF16),
            heavy,
            input_output_aliases={5: 0},
        )(t, meta, queries, w, target, out)

    def both(i, carry):
        chunk0, m0, pair1, scale1, m1, out = carry
        t = jnp.reshape(i, (1,))
        got1 = reduce(pair1)
        w0 = gather(chunk0)
        pair0, scale0 = sums(0, t, 0, w0)
        out = answer(0, t, 1, w0, out)
        got1, pair0 = lax.optimization_barrier((got1, pair0))
        chunk1, m1 = update(got1, m1, scale1)
        got0 = reduce(pair0)
        w1 = gather(chunk1)
        pair1, scale1 = sums(1, t, -1, w1)
        out = answer(1, t, 0, w1, out)
        chunk0, m0 = update(got0, m0, scale0)
        return chunk0, m0, pair1, scale1, m1, out

    def one(i, carry):
        chunk, m, out = carry
        t = jnp.reshape(i, (1,))
        w = gather(chunk)
        pair, scale = sums(0, t, 0, w)
        got = reduce(pair)
        out = answer(0, t, 1, w, out)
        chunk, m = update(got, m, scale)
        return chunk, m, out

    out = jnp.zeros(flat, BF16)
    pair1, scale1 = sums(1, jnp.zeros((1,), jnp.int32), 0, w_init)
    chunk0, m0, _, _, _, out = lax.fori_loop(0, shortest, both, (chunk, m_init, pair1, scale1, m_init, out))
    chunk0, _, out = lax.fori_loop(shortest, longest, one, (chunk0, m0, out))
    out = answer(0, jnp.reshape(longest, (1,)), 1, gather(chunk0), out)
    return out.reshape(slots, blocks, block_rows, width)


def solution(mesh):
    seq, head, rows = (mesh.shape[name] for name in ("seq", "head", "rows"))
    split = Mesh(mesh.devices.reshape(seq, head, rows // 2, 2), ("seq", "head", "z", "core"))
    data = P("seq", None, ("z", "core"), "head")
    weight = P("head", None, None)
    return jax.shard_map(
        body,
        mesh=split,
        in_specs=(data, data, data, P(), P("head"), weight, weight, weight),
        out_specs=data,
        check_vma=False,
    )
```

time: 250 us -> 336 us (1.34)
  the two profiles are of different devices: /device:TPU:5 before, /device:TPU:7 now
where the time goes in v2:
time: 336 us; the launch traced here: 334 us
  blocking collectives  186 us (55%)
  Pallas kernels  56.2 us (17%)
  starting transfers between devices  45.5 us (14%)
  waiting for transfers between devices  28.2 us (8%)
  other arithmetic  7.82 us (2%)
  local copies, waits for them, and re-layouts  5.92 us (2%)
  loops' own time  4.32 us (1%)
    all_gather x9, blocking collectives, gather(): return lax.all_gather(chunk, ('z', 'core'), axis=0)  186 us
    all_to_all x8, starting transfers between devices, reduce(): return lax.all_to_all(pair, 'z', 0, 0, tiled=True)  41.7 us
    pallas_call x9, Pallas kernels, sums(): call(sums_kernel, 2, [row_block(chain, shift), row_block(chain, shift), w...  30 us
    pallas_call x9, Pallas kernels, answer(): call(functools.partial(answer_kernel, chain=chain, shift=shift), 2, [row_...  23.2 us
    all_to_all x8, waiting for transfers between devices, reduce(): return lax.all_to_all(pair, 'z', 0, 0, tiled=True)  21.8 us
    convert_element_type x9, other arithmetic, sums(): return ((keep.astype(F32) + got.astype(F32)).astype(BF16), scale)  7.82 us
  transfers between devices with their start and end apart: 17, of which 9 were waited for; matrix products, arithmetic and copies ran while one was open for 2% of the time, Pallas kernels for 14%

profile of v2, /device:TPU:7, one launch (start us, length us, event | category | flops | bytes accessed | tf_op | source)
XLA Modules:
  0.0 334.2 jit_solution(5329380248449175583)
XLA Ops:
  1.0 0.9 copy-done.1
  3.5 1.4 shard_map.82
  4.9 3.3 shard_map.83
  11.2 1.7 broadcast_in_dim.3
  12.9 299.4 %while.34 = (s32[]{:T(128)}, bf16[3,16,512]{2,1,0:T(8,128)(2,1)S(1)}, f32[3,16,512]{2,1,0:T(8,128)S(1)}, bf16[8,3,16,512]{3,2,1,0:T(8,128)(2,1)}, f32[1,512]{1,0...) while((s32[]{:T(128)}, ...), condition=%wide.region_1.0_spmd, body=%wide.region_0.0_spmd.sunk | while | flops 2014838784 | bytes 45580616 | solution.py:229
  13.5 8.2 %all-to-all-start = ((bf16[8,3,16,512]{3,2,1,0:T(8,128)(2,1)}), bf16[8,3,16,512]{3,2,1,0:T(8,128)(2,1)S(1)}, u32[]{:S(2)}, u32[]{:S(2)}) async-start(bf16[8,3,16,512]{3,2,1,0:T(8,128)(2,1)} %get-tuple-element.464), calls=%async_computation | async-start | bytes 786432 | tf_op jit(solution)/shard_map/while/body/all_to_all | solution.py:176
  21.7 25.3 %all-gather.7 = bf16[48,16,512]{2,1,0:T(8,128)(2,1)S(1)} all-gather(bf16[3,16,512]{2,1,0:T(8,128)(2,1)S(1)} %get-tuple-element.462), channel_id=2, replica_groups=mesh['seq'=4,'head'=4,'z'=8,'core'=2] {'z','core'}, dimensions={0}, use_global_device_ids=true | all-gather | bytes 835584 | tf_op jit(solution)/shard_map/while/body/all_gather | solution.py:188
  47.0 3.3 body.9
  50.6 1.6 collective-permute-done
  53.2 16.8 %all-gather.8 = bf16[48,16,512]{2,1,0:T(8,128)(2,1)S(1)} all-gather(bf16[3,16,512]{2,1,0:T(8,128)(2,1)S(1)} %get-tuple-element.423), channel_id=3, replica_groups=mesh['seq'=4,'head'=4,'z'=8,'core'=2] {'z','core'}, dimensions={0}, use_global_device_ids=true | all-gather | bytes 835584 | tf_op jit(solution)/shard_map/while/body/all_gather | solution.py:188
  70.1 5.8 %all-to-all-start.1 = ((bf16[8,3,16,512]{3,2,1,0:T(8,128)(2,1)}), bf16[8,3,16,512]{3,2,1,0:T(8,128)(2,1)S(1)}, u32[]{:S(2)}, u32[]{:S(2)}) async-start(bf16[8,3,16,512]{3,2,1,0:T(8,128)(2,1)} %add_convert_fusion.7), calls=%async_computation.1 | async-start | bytes 786432 | tf_op jit(solution)/shard_map/while/body/all_to_all | solution.py:176
  75.8 3.3 %body.12 = (bf16[8,3,16,512]{3,2,1,0:T(8,128)(2,1)S(1)}, bf16[8,3,16,512]{3,2,1,0:T(8,128)(2,1)S(1)}, f32[1,512]{1,0:T(1,128)S(1)}) custom-call(s32[1]{0:T(128)} %bitcast.17.t, s32[8]{0:T(128)S(1)} %get-tuple-element.485.meta, bf16[8,320,512]{2,1,0:T(8,128)(2,1)} %get-tuple-element.486.k_ref, bf16[8,320,512]{2,1,0:T(8,128)(2,1)} %get-tuple-element.487.v_ref, ...), custom_call_target="tpu_custom_call" | custom-call | flops 503316480 | bytes 6291456 | tf_op jit(solution)/shard_map/while/body/pallas_call | solution.py:164
  79.7 2.5 body.13.old_ref
  82.2 1.9 body.14
  85.1 5.9 %all-to-all-done.1.x_ref = bf16[8,3,16,512]{3,2,1,0:T(8,128)(2,1)S(1)} async-done(((bf16[8,3,16,512]{3,2,1,0:T(8,128)(2,1)}), bf16[8,3,16,512]{3,2,1,0:T(8,128)(2,1)S(1)}, u32[]{:S(2)}, u32[]{:S(2)}) %all-to-all-start.1) | async-done | bytes 393248 | tf_op jit(solution)/shard_map/while/body/all_to_all | solution.py:176
  91.8 3.5 %all-to-all-start = ((bf16[8,3,16,512]{3,2,1,0:T(8,128)(2,1)}), bf16[8,3,16,512]{3,2,1,0:T(8,128)(2,1)S(1)}, u32[]{:S(2)}, u32[]{:S(2)}) async-start(bf16[8,3,16,512]{3,2,1,0:T(8,128)(2,1)} %get-tuple-element.464), calls=%async_computation | async-start | bytes 786432 | tf_op jit(solution)/shard_map/while/body/all_to_all | solution.py:176
  95.3 25.2 %all-gather.7 = bf16[48,16,512]{2,1,0:T(8,128)(2,1)S(1)} all-gather(bf16[3,16,512]{2,1,0:T(8,128)(2,1)S(1)} %get-tuple-element.462), channel_id=2, replica_groups=mesh['seq'=4,'head'=4,'z'=8,'core'=2] {'z','core'}, dimensions={0}, use_global_device_ids=true | all-gather | bytes 835584 | tf_op jit(solution)/shard_map/while/body/all_gather | solution.py:188
  120.5 3.3 body.9
  124.1 1.6 collective-permute-done
  126.7 16.9 %all-gather.8 = bf16[48,16,512]{2,1,0:T(8,128)(2,1)S(1)} all-gather(bf16[3,16,512]{2,1,0:T(8,128)(2,1)S(1)} %get-tuple-element.423), channel_id=3, replica_groups=mesh['seq'=4,'head'=4,'z'=8,'core'=2] {'z','core'}, dimensions={0}, use_global_device_ids=true | all-gather | bytes 835584 | tf_op jit(solution)/shard_map/while/body/all_gather | solution.py:188
  143.6 5.8 %all-to-all-start.1 = ((bf16[8,3,16,512]{3,2,1,0:T(8,128)(2,1)}), bf16[8,3,16,512]{3,2,1,0:T(8,128)(2,1)S(1)}, u32[]{:S(2)}, u32[]{:S(2)}) async-start(bf16[8,3,16,512]{3,2,1,0:T(8,128)(2,1)} %add_convert_fusion.7), calls=%async_computation.1 | async-start | bytes 786432 | tf_op jit(solution)/shard_map/while/body/all_to_all | solution.py:176
  149.3 3.3 %body.12 = (bf16[8,3,16,512]{3,2,1,0:T(8,128)(2,1)S(1)}, bf16[8,3,16,512]{3,2,1,0:T(8,128)(2,1)S(1)}, f32[1,512]{1,0:T(1,128)S(1)}) custom-call(s32[1]{0:T(128)} %bitcast.17.t, s32[8]{0:T(128)S(1)} %get-tuple-element.485.meta, bf16[8,320,512]{2,1,0:T(8,128)(2,1)} %get-tuple-element.486.k_ref, bf16[8,320,512]{2,1,0:T(8,128)(2,1)} %get-tuple-element.487.v_ref, ...), custom_call_target="tpu_custom_call" | custom-call | flops 503316480 | bytes 6291456 | tf_op jit(solution)/shard_map/while/body/pallas_call | solution.py:164
  153.2 3.1 body.13.old_ref
  156.4 1.9 body.14
  159.2 5.3 %all-to-all-done.1.x_ref = bf16[8,3,16,512]{3,2,1,0:T(8,128)(2,1)S(1)} async-done(((bf16[8,3,16,512]{3,2,1,0:T(8,128)(2,1)}), bf16[8,3,16,512]{3,2,1,0:T(8,128)(2,1)S(1)}, u32[]{:S(2)}, u32[]{:S(2)}) %all-to-all-start.1) | async-done | bytes 393248 | tf_op jit(solution)/shard_map/while/body/all_to_all | solution.py:176
  165.3 3.5 %all-to-all-start = ((bf16[8,3,16,512]{3,2,1,0:T(8,128)(2,1)}), bf16[8,3,16,512]{3,2,1,0:T(8,128)(2,1)S(1)}, u32[]{:S(2)}, u32[]{:S(2)}) async-start(bf16[8,3,16,512]{3,2,1,0:T(8,128)(2,1)} %get-tuple-element.464), calls=%async_computation | async-start | bytes 786432 | tf_op jit(solution)/shard_map/while/body/all_to_all | solution.py:176
  168.8 25.2 %all-gather.7 = bf16[48,16,512]{2,1,0:T(8,128)(2,1)S(1)} all-gather(bf16[3,16,512]{2,1,0:T(8,128)(2,1)S(1)} %get-tuple-element.462), channel_id=2, replica_groups=mesh['seq'=4,'head'=4,'z'=8,'core'=2] {'z','core'}, dimensions={0}, use_global_device_ids=true | all-gather | bytes 835584 | tf_op jit(solution)/shard_map/while/body/all_gather | solution.py:188
  194.0 3.3 body.9
  197.6 1.6 collective-permute-done
  200.2 16.9 %all-gather.8 = bf16[48,16,512]{2,1,0:T(8,128)(2,1)S(1)} all-gather(bf16[3,16,512]{2,1,0:T(8,128)(2,1)S(1)} %get-tuple-element.423), channel_id=3, replica_groups=mesh['seq'=4,'head'=4,'z'=8,'core'=2] {'z','core'}, dimensions={0}, use_global_device_ids=true | all-gather | bytes 835584 | tf_op jit(solution)/shard_map/while/body/all_gather | solution.py:188
  217.1 5.8 %all-to-all-start.1 = ((bf16[8,3,16,512]{3,2,1,0:T(8,128)(2,1)}), bf16[8,3,16,512]{3,2,1,0:T(8,128)(2,1)S(1)}, u32[]{:S(2)}, u32[]{:S(2)}) async-start(bf16[8,3,16,512]{3,2,1,0:T(8,128)(2,1)} %add_convert_fusion.7), calls=%async_computation.1 | async-start | bytes 786432 | tf_op jit(solution)/shard_map/while/body/all_to_all | solution.py:176
  222.9 3.3 %body.12 = (bf16[8,3,16,512]{3,2,1,0:T(8,128)(2,1)S(1)}, bf16[8,3,16,512]{3,2,1,0:T(8,128)(2,1)S(1)}, f32[1,512]{1,0:T(1,128)S(1)}) custom-call(s32[1]{0:T(128)} %bitcast.17.t, s32[8]{0:T(128)S(1)} %get-tuple-element.485.meta, bf16[8,320,512]{2,1,0:T(8,128)(2,1)} %get-tuple-element.486.k_ref, bf16[8,320,512]{2,1,0:T(8,128)(2,1)} %get-tuple-element.487.v_ref, ...), custom_call_target="tpu_custom_call" | custom-call | flops 503316480 | bytes 6291456 | tf_op jit(solution)/shard_map/while/body/pallas_call | solution.py:164
  226.8 3.1 body.13.old_ref
  229.9 1.9 body.14
  232.7 5.3 %all-to-all-done.1.x_ref = bf16[8,3,16,512]{3,2,1,0:T(8,128)(2,1)S(1)} async-done(((bf16[8,3,16,512]{3,2,1,0:T(8,128)(2,1)}), bf16[8,3,16,512]{3,2,1,0:T(8,128)(2,1)S(1)}, u32[]{:S(2)}, u32[]{:S(2)}) %all-to-all-start.1) | async-done | bytes 393248 | tf_op jit(solution)/shard_map/while/body/all_to_all | solution.py:176
  238.8 3.5 %all-to-all-start = ((bf16[8,3,16,512]{3,2,1,0:T(8,128)(2,1)}), bf16[8,3,16,512]{3,2,1,0:T(8,128)(2,1)S(1)}, u32[]{:S(2)}, u32[]{:S(2)}) async-start(bf16[8,3,16,512]{3,2,1,0:T(8,128)(2,1)} %get-tuple-element.464), calls=%async_computation | async-start | bytes 786432 | tf_op jit(solution)/shard_map/while/body/all_to_all | solution.py:176
  242.3 25.2 %all-gather.7 = bf16[48,16,512]{2,1,0:T(8,128)(2,1)S(1)} all-gather(bf16[3,16,512]{2,1,0:T(8,128)(2,1)S(1)} %get-tuple-element.462), channel_id=2, replica_groups=mesh['seq'=4,'head'=4,'z'=8,'core'=2] {'z','core'}, dimensions={0}, use_global_device_ids=true | all-gather | bytes 835584 | tf_op jit(solution)/shard_map/while/body/all_gather | solution.py:188
  267.5 3.3 body.9
  271.1 1.6 collective-permute-done
  273.7 16.9 %all-gather.8 = bf16[48,16,512]{2,1,0:T(8,128)(2,1)S(1)} all-gather(bf16[3,16,512]{2,1,0:T(8,128)(2,1)S(1)} %get-tuple-element.423), channel_id=3, replica_groups=mesh['seq'=4,'head'=4,'z'=8,'core'=2] {'z','core'}, dimensions={0}, use_global_device_ids=true | all-gather | bytes 835584 | tf_op jit(solution)/shard_map/while/body/all_gather | solution.py:188
  290.6 5.8 %all-to-all-start.1 = ((bf16[8,3,16,512]{3,2,1,0:T(8,128)(2,1)}), bf16[8,3,16,512]{3,2,1,0:T(8,128)(2,1)S(1)}, u32[]{:S(2)}, u32[]{:S(2)}) async-start(bf16[8,3,16,512]{3,2,1,0:T(8,128)(2,1)} %add_convert_fusion.7), calls=%async_computation.1 | async-start | bytes 786432 | tf_op jit(solution)/shard_map/while/body/all_to_all | solution.py:176
  296.4 3.3 %body.12 = (bf16[8,3,16,512]{3,2,1,0:T(8,128)(2,1)S(1)}, bf16[8,3,16,512]{3,2,1,0:T(8,128)(2,1)S(1)}, f32[1,512]{1,0:T(1,128)S(1)}) custom-call(s32[1]{0:T(128)} %bitcast.17.t, s32[8]{0:T(128)S(1)} %get-tuple-element.485.meta, bf16[8,320,512]{2,1,0:T(8,128)(2,1)} %get-tuple-element.486.k_ref, bf16[8,320,512]{2,1,0:T(8,128)(2,1)} %get-tuple-element.487.v_ref, ...), custom_call_target="tpu_custom_call" | custom-call | flops 503316480 | bytes 6291456 | tf_op jit(solution)/shard_map/while/body/pallas_call | solution.py:164
  300.3 3.1 body.13.old_ref
  303.4 1.9 body.14
  306.2 5.3 %all-to-all-done.1.x_ref = bf16[8,3,16,512]{3,2,1,0:T(8,128)(2,1)S(1)} async-done(((bf16[8,3,16,512]{3,2,1,0:T(8,128)(2,1)}), bf16[8,3,16,512]{3,2,1,0:T(8,128)(2,1)S(1)}, u32[]{:S(2)}, u32[]{:S(2)}) %all-to-all-start.1) | async-done | bytes 393248 | tf_op jit(solution)/shard_map/while/body/all_to_all | solution.py:176
  312.3 1.2 while.35
  313.5 17.2 %all-gather.3 = bf16[48,16,512]{2,1,0:T(8,128)(2,1)S(1)} all-gather(bf16[3,16,512]{2,1,0:T(8,128)(2,1)S(1)} %get-tuple-element.187), channel_id=5, replica_groups=mesh['seq'=4,'head'=4,'z'=8,'core'=2] {'z','core'}, dimensions={0}, use_global_device_ids=true | all-gather | bytes 835584 | tf_op jit(solution)/shard_map/all_gather | solution.py:188
  330.7 3.5 %shard_map.84 = bf16[8,320,512]{2,1,0:T(8,128)(2,1)} custom-call(s32[1]{0:T(128)} %get-tuple-element.244.t, s32[8]{0:T(128)S(1)} %get-tuple-element.550, bf16[8,320,512]{2,1,0:T(8,128)(2,1)} %get-tuple-element.540, bf16[16,3,16,512]{3,2,1,0:T(8,128)(2,1)S(1)} %bitcast.28, f32[1,512]{1,0:T(1,128)S(1)} %get-tuple-element.548, ...), custom_call_target="tpu_custom_call", output_to_operand_aliasing={{}: (5, {})} | custom-call | flops 503316480 | bytes 6291456 | tf_op jit(solution)/shard_map/pallas_call | solution.py:191
  (60 shorter events, 16.6 us)
Async XLA Ops:
  0.0 0.9 copy-start
  1.0 0.9 copy-start.1
  1.9 0.9 copy-start.2
  2.9 0.7 copy-start.3
  8.2 2.1 collective-permute-start.3
  13.5 39.5 %all-to-all-start = ((bf16[8,3,16,512]{3,2,1,0:T(8,128)(2,1)}), bf16[8,3,16,512]{3,2,1,0:T(8,128)(2,1)S(1)}, u32[]{:S(2)}, u32[]{:S(2)}) async-start(bf16[8,3,16,512]{3,2,1,0:T(8,128)(2,1)} %get-tuple-element.464), calls=%async_computation | async-start | bytes 786432 | tf_op jit(solution)/shard_map/while/body/all_to_all | solution.py:176
  50.3 1.8 collective-permute-start
  70.1 20.9 %all-to-all-start.1 = ((bf16[8,3,16,512]{3,2,1,0:T(8,128)(2,1)}), bf16[8,3,16,512]{3,2,1,0:T(8,128)(2,1)S(1)}, u32[]{:S(2)}, u32[]{:S(2)}) async-start(bf16[8,3,16,512]{3,2,1,0:T(8,128)(2,1)} %add_convert_fusion.7), calls=%async_computation.1 | async-start | bytes 786432 | tf_op jit(solution)/shard_map/while/body/all_to_all | solution.py:176
  79.2 5.0 %collective-permute-start.1 = (bf16[8,3,16,512]{3,2,1,0:T(8,128)(2,1)S(1)}, bf16[8,3,16,512]{3,2,1,0:T(8,128)(2,1)S(1)}, u32[]{:S(2)}, u32[]{:S(2)}) collective-permute-start(bf16[8,3,16,512]{3,2,1,0:T(8,128)(2,1)S(1)} %get-tuple-element.424), channel_id=1, source_target_pairs={{0,1},{1,0},{2,3},{3,2},{4,5},{5,4},{6,7},{7,6},{8,9},{9,8},{10,11... | collective-permute-start | bytes 1179656 | tf_op jit(solution)/shard_map/while/body/ppermute | solution.py:172
  79.7 2.5 copy-start.4
  91.8 34.7 %all-to-all-start = ((bf16[8,3,16,512]{3,2,1,0:T(8,128)(2,1)}), bf16[8,3,16,512]{3,2,1,0:T(8,128)(2,1)S(1)}, u32[]{:S(2)}, u32[]{:S(2)}) async-start(bf16[8,3,16,512]{3,2,1,0:T(8,128)(2,1)} %get-tuple-element.464), calls=%async_computation | async-start | bytes 786432 | tf_op jit(solution)/shard_map/while/body/all_to_all | solution.py:176
  123.8 1.8 collective-permute-start
  143.6 20.9 %all-to-all-start.1 = ((bf16[8,3,16,512]{3,2,1,0:T(8,128)(2,1)}), bf16[8,3,16,512]{3,2,1,0:T(8,128)(2,1)S(1)}, u32[]{:S(2)}, u32[]{:S(2)}) async-start(bf16[8,3,16,512]{3,2,1,0:T(8,128)(2,1)} %add_convert_fusion.7), calls=%async_computation.1 | async-start | bytes 786432 | tf_op jit(solution)/shard_map/while/body/all_to_all | solution.py:176
  152.7 5.6 %collective-permute-start.1 = (bf16[8,3,16,512]{3,2,1,0:T(8,128)(2,1)S(1)}, bf16[8,3,16,512]{3,2,1,0:T(8,128)(2,1)S(1)}, u32[]{:S(2)}, u32[]{:S(2)}) collective-permute-start(bf16[8,3,16,512]{3,2,1,0:T(8,128)(2,1)S(1)} %get-tuple-element.424), channel_id=1, source_target_pairs={{0,1},{1,0},{2,3},{3,2},{4,5},{5,4},{6,7},{7,6},{8,9},{9,8},{10,11... | collective-permute-start | bytes 1179656 | tf_op jit(solution)/shard_map/while/body/ppermute | solution.py:172
  153.2 3.1 copy-start.4
  165.3 34.7 %all-to-all-start = ((bf16[8,3,16,512]{3,2,1,0:T(8,128)(2,1)}), bf16[8,3,16,512]{3,2,1,0:T(8,128)(2,1)S(1)}, u32[]{:S(2)}, u32[]{:S(2)}) async-start(bf16[8,3,16,512]{3,2,1,0:T(8,128)(2,1)} %get-tuple-element.464), calls=%async_computation | async-start | bytes 786432 | tf_op jit(solution)/shard_map/while/body/all_to_all | solution.py:176
  197.3 1.8 collective-permute-start
  217.1 20.9 %all-to-all-start.1 = ((bf16[8,3,16,512]{3,2,1,0:T(8,128)(2,1)}), bf16[8,3,16,512]{3,2,1,0:T(8,128)(2,1)S(1)}, u32[]{:S(2)}, u32[]{:S(2)}) async-start(bf16[8,3,16,512]{3,2,1,0:T(8,128)(2,1)} %add_convert_fusion.7), calls=%async_computation.1 | async-start | bytes 786432 | tf_op jit(solution)/shard_map/while/body/all_to_all | solution.py:176
  226.2 5.6 %collective-permute-start.1 = (bf16[8,3,16,512]{3,2,1,0:T(8,128)(2,1)S(1)}, bf16[8,3,16,512]{3,2,1,0:T(8,128)(2,1)S(1)}, u32[]{:S(2)}, u32[]{:S(2)}) collective-permute-start(bf16[8,3,16,512]{3,2,1,0:T(8,128)(2,1)S(1)} %get-tuple-element.424), channel_id=1, source_target_pairs={{0,1},{1,0},{2,3},{3,2},{4,5},{5,4},{6,7},{7,6},{8,9},{9,8},{10,11... | collective-permute-start | bytes 1179656 | tf_op jit(solution)/shard_map/while/body/ppermute | solution.py:172
  226.7 3.1 copy-start.4
  238.8 34.7 %all-to-all-start = ((bf16[8,3,16,512]{3,2,1,0:T(8,128)(2,1)}), bf16[8,3,16,512]{3,2,1,0:T(8,128)(2,1)S(1)}, u32[]{:S(2)}, u32[]{:S(2)}) async-start(bf16[8,3,16,512]{3,2,1,0:T(8,128)(2,1)} %get-tuple-element.464), calls=%async_computation | async-start | bytes 786432 | tf_op jit(solution)/shard_map/while/body/all_to_all | solution.py:176
  270.8 1.8 collective-permute-start
  290.6 20.9 %all-to-all-start.1 = ((bf16[8,3,16,512]{3,2,1,0:T(8,128)(2,1)}), bf16[8,3,16,512]{3,2,1,0:T(8,128)(2,1)S(1)}, u32[]{:S(2)}, u32[]{:S(2)}) async-start(bf16[8,3,16,512]{3,2,1,0:T(8,128)(2,1)} %add_convert_fusion.7), calls=%async_computation.1 | async-start | bytes 786432 | tf_op jit(solution)/shard_map/while/body/all_to_all | solution.py:176
  299.7 5.6 %collective-permute-start.1 = (bf16[8,3,16,512]{3,2,1,0:T(8,128)(2,1)S(1)}, bf16[8,3,16,512]{3,2,1,0:T(8,128)(2,1)S(1)}, u32[]{:S(2)}, u32[]{:S(2)}) collective-permute-start(bf16[8,3,16,512]{3,2,1,0:T(8,128)(2,1)S(1)} %get-tuple-element.424), channel_id=1, source_target_pairs={{0,1},{1,0},{2,3},{3,2},{4,5},{5,4},{6,7},{7,6},{8,9},{9,8},{10,11... | collective-permute-start | bytes 1179656 | tf_op jit(solution)/shard_map/while/body/ppermute | solution.py:172
  300.2 3.1 copy-start.4
